TPU v7x, 32 devices: a whole 2x2x4 slice. The times are simulated.
32 devices in a mesh: dp: 4 (over x, core), seq: 2 (over y), fsdp: 4 (over z).
Axes of the slice: x: 2, y: 2, z: 4, core: 2. Of those that a mesh axis runs over, the one named last changes fastest.
Arguments:
- tokens: bfloat16 [16, 1536, 768], P(('dp', 'fsdp'), 'seq'), may hold values from -6 to 6
- attn_in: bfloat16 [768, 2304], P('fsdp'), may hold values from -0.21875 to 0.21875
- attn_out: bfloat16 [768, 768], P('fsdp'), may hold values from -1.75 to 1.75
- router: bfloat16 [768, 4], P('fsdp'), may hold values from -0.15625 to 0.15625
- gains: bfloat16 [768, 2], P('fsdp'), may hold values from 0.5 to 1.5
- expert_w: bfloat16 [3072, 4, 1536], P('fsdp'), may hold values from -0.21875 to 0.21875
- expert_ids: int32 [16, 1536, 2], P(('dp', 'fsdp'), 'seq'), may hold values from 0 to 3, all different within a row
- segments: int32 [16, 512], P(('dp', 'fsdp')), may hold values from 0 to 1, as said below
- cotangent: bfloat16 [16, 1536, 768], P(('dp', 'fsdp'), 'seq'), may hold values from -6 to 6
Outputs:
- block_out: bfloat16 [16, 1536, 768], P(('dp', 'fsdp'), 'seq')
- d_tokens: bfloat16 [16, 1536, 768], P(('dp', 'fsdp'), 'seq')
- d_attn_in: float32 [768, 2304], P('fsdp')
- d_attn_out: float32 [768, 768], P('fsdp')
- d_router: float32 [768, 4], P('fsdp')
- d_gains: float32 [768, 2], P('fsdp')
- d_expert: float32 [3072, 4, 1536], P('fsdp')
Inputs may be any that keep to these rules, and one draw needn't show every extreme that they name: `expert_ids`: the two experts of a token differ. `segments`: never falls along a group; every continuation has 64 to 384 tokens, and in every group one has exactly 384.
All inputs are finite; a program needn't handle non-finite values.
Results may differ from a plain program's by a relative error of at most 0.018.
Values may be sent and summed in bfloat16 or wider, within the bound.
A program may use at most 384 MiB of HBM per device.

v0:
```python
import jax
import jax.numpy as jnp
from jax import lax
from jax.sharding import PartitionSpec as P

HEADS = 12
HEAD_DIM = 64
EXPERTS = 4
PROMPT = 1024
EPSILON = 1e-06
NEGATIVE = -1e30
HIGH = lax.Precision.HIGHEST


def route(choose, capacity, experts_count):
    pair_expert = choose.reshape(-1)
    one_hot = (pair_expert[:, None] == jnp.arange(experts_count, dtype=jnp.int32)[None, :]).astype(
        jnp.int32
    )
    before = jnp.cumsum(one_hot, axis=0) - one_hot
    place = jnp.sum(before * one_hot, axis=1)
    kept = place < capacity
    slots = jnp.where(kept, pair_expert * capacity + place, experts_count * capacity)
    pair_count = pair_expert.shape[0]
    pair_of = (
        jnp.zeros((experts_count * capacity + 1,), jnp.int32)
        .at[slots]
        .set(jnp.arange(pair_count, dtype=jnp.int32))
    )
    filled = (
        jnp.zeros((experts_count * capacity + 1,), jnp.int32)
        .at[slots]
        .set(jnp.ones((pair_count,), jnp.int32))
    )
    return (slots, kept, pair_of[:-1], filled[:-1] > 0)


def expert_pre(expert_in, piece):
    width = piece.shape[2] // 2
    return jnp.einsum(
        "ecd,fed->ecf", expert_in, piece[:, :, :width], preferred_element_type=jnp.float32
    )


def expert_out(activity, piece):
    width = piece.shape[2] // 2
    return jnp.einsum(
        "ecf,fed->ecd", activity, piece[:, :, width:], preferred_element_type=jnp.float32
    )


def expert_back(grad_result, pre_rows, piece):
    width = piece.shape[2] // 2
    grad_act = jnp.einsum(
        "ecd,fed->ecf", grad_result, piece[:, :, width:], preferred_element_type=jnp.float32
    )
    grad_pre = jax.vjp(jax.nn.gelu, pre_rows)[1](grad_act)[0].astype(jnp.bfloat16)
    grad_in = jnp.einsum(
        "ecf,fed->ecd", grad_pre, piece[:, :, :width], preferred_element_type=jnp.float32
    )
    return (grad_pre, grad_in)


def shards(tokens, attn_in, attn_out, router, gains, expert_w, expert_ids, segments, cotangent):
    x_rows = tokens[0].astype(jnp.float32)
    tok_rows = x_rows.shape[0]
    width = x_rows.shape[1]
    seq_count = lax.axis_size("seq")
    scale = HEAD_DIM ** (-0.5)
    w_qkv, w_proj, w_route, gain_pair = (
        lax.all_gather(attn_in, "fsdp", axis=0, tiled=True),
        lax.all_gather(attn_out, "fsdp", axis=0, tiled=True),
        lax.all_gather(router, "fsdp", axis=0, tiled=True),
        lax.all_gather(gains, "fsdp", axis=0, tiled=True),
    )
    gain_f = gain_pair.astype(jnp.float32)
    r_one = lax.rsqrt(jnp.mean(x_rows * x_rows, axis=-1, keepdims=True) + EPSILON)
    normed_one = x_rows * r_one
    normed_low = (normed_one * gain_f[:, 0]).astype(jnp.bfloat16)
    projected = jnp.dot(normed_low, w_qkv, preferred_element_type=jnp.float32).astype(jnp.bfloat16)
    local_heads = HEADS // seq_count
    head_cols = local_heads * HEAD_DIM
    arrived = lax.all_to_all(
        projected.reshape(tok_rows, 3, seq_count, head_cols),
        "seq",
        split_axis=2,
        concat_axis=0,
        tiled=True,
    )
    group_len = arrived.shape[0]
    queries = arrived[:, 0, 0].reshape(group_len, local_heads, HEAD_DIM)
    keys = arrived[:, 1, 0].reshape(group_len, local_heads, HEAD_DIM)
    values = arrived[:, 2, 0].reshape(group_len, local_heads, HEAD_DIM)
    seg_full = jnp.concatenate([jnp.full((PROMPT,), -1, jnp.int32), segments[0]])
    block = min(512, group_len)
    key_place = jnp.arange(group_len, dtype=jnp.int32)
    begins = jnp.arange(group_len // block, dtype=jnp.int32) * block

    def block_scores(begin):
        query_block = lax.dynamic_slice_in_dim(queries, begin, block, 0)
        query_place = begin + jnp.arange(block, dtype=jnp.int32)
        query_seg = lax.dynamic_slice_in_dim(seg_full, begin, block, 0)
        raw = (
            jnp.einsum("qhd,khd->hqk", query_block, keys, preferred_element_type=jnp.float32)
            * scale
        )
        allowed = (key_place[None, :] <= query_place[:, None]) & (
            (seg_full[None, :] < 0) | (seg_full[None, :] == query_seg[:, None])
        )
        return (jnp.where(allowed[None], raw, NEGATIVE), query_block)

    def forward_block(begin):
        masked, query_block = block_scores(begin)
        row_max = jnp.max(masked, axis=-1, keepdims=True)
        expo = jnp.exp(masked - row_max)
        row_total = jnp.sum(expo, axis=-1, keepdims=True)
        probs = expo / row_total
        mixed_block = jnp.einsum(
            "hqk,khd->qhd", probs.astype(jnp.bfloat16), values, preferred_element_type=jnp.float32
        )
        return (mixed_block.astype(jnp.bfloat16), (row_max + jnp.log(row_total))[:, :, 0])

    mixed_blocks, log_totals = lax.map(forward_block, begins)
    mixed_heads = mixed_blocks.reshape(group_len, 1, head_cols)
    returned = lax.all_to_all(mixed_heads, "seq", split_axis=0, concat_axis=1, tiled=True)
    attended = returned.reshape(tok_rows, width)
    hidden = x_rows + jnp.dot(attended, w_proj, preferred_element_type=jnp.float32)
    r_two = lax.rsqrt(jnp.mean(hidden * hidden, axis=-1, keepdims=True) + EPSILON)
    normed_two = hidden * r_two
    routed_low = (normed_two * gain_f[:, 1]).astype(jnp.bfloat16)
    logits = jnp.dot(routed_low, w_route, preferred_element_type=jnp.float32)
    probs_r = jax.nn.softmax(logits, axis=-1)
    choose = expert_ids[0]
    choose_map = (choose[:, :, None] == jnp.arange(EXPERTS, dtype=jnp.int32)[None, None, :]).astype(
        jnp.float32
    )
    gates = jnp.sum(probs_r[:, None, :] * choose_map, axis=-1)
    capacity = 2 * tok_rows // EXPERTS
    slots, kept, pair_of, filled = route(choose, capacity, EXPERTS)
    token_of = pair_of // 2
    expert_in = jnp.where(
        filled[:, None], routed_low[token_of], jnp.zeros((), jnp.bfloat16)
    ).reshape(EXPERTS, capacity, width)
    piece = lax.all_gather(expert_w, "fsdp", axis=0, tiled=True)
    pre_rows = expert_pre(expert_in, piece)
    result = expert_out(jax.nn.gelu(pre_rows).astype(jnp.bfloat16), piece)
    padded = jnp.concatenate(
        [result.reshape(EXPERTS * capacity, width), jnp.zeros((1, width), jnp.float32)], axis=0
    )
    picked = padded[slots].reshape(tok_rows, 2, width)
    kept_f = kept.astype(jnp.float32).reshape(tok_rows, 2)
    weight_pair = gates * kept_f
    block_out = hidden + jnp.sum(weight_pair[..., None] * picked, axis=1)
    grad_out_rows = cotangent[0].astype(jnp.float32)
    grad_gates = kept_f * jnp.sum(grad_out_rows[:, None, :] * picked, axis=-1)
    grad_probs = jnp.sum(grad_gates[:, :, None] * choose_map, axis=1)
    grad_logits = probs_r * (grad_probs - jnp.sum(probs_r * grad_probs, axis=-1, keepdims=True))
    grad_route_w = jnp.dot(routed_low.astype(jnp.float32).T, grad_logits, precision=HIGH)
    grad_routed = jnp.dot(grad_logits, w_route.astype(jnp.float32).T, precision=HIGH)
    scaled = (weight_pair[:, :, None] * grad_out_rows[:, None, :]).reshape(2 * tok_rows, width)
    grad_result = (
        jnp.where(filled[:, None], scaled[pair_of], 0.0)
        .astype(jnp.bfloat16)
        .reshape(EXPERTS, capacity, width)
    )
    piece = lax.all_gather(expert_w, "fsdp", axis=0, tiled=True)
    pre_rows = expert_pre(expert_in, piece)
    act_rows = jax.nn.gelu(pre_rows).astype(jnp.bfloat16)
    grad_pre_rows, grad_in_rows = expert_back(grad_result, pre_rows, piece)
    act_store = act_rows
    pre_rows = grad_pre_rows
    act_rows = act_store
    grad_first = jnp.einsum("ecd,ecf->fed", expert_in, pre_rows, preferred_element_type=jnp.float32)
    grad_second = jnp.einsum(
        "ecf,ecd->fed", act_rows, grad_result, preferred_element_type=jnp.float32
    )
    expert_shard = lax.psum_scatter(
        jnp.concatenate([grad_first, grad_second], axis=2).astype(jnp.bfloat16),
        "fsdp",
        scatter_dimension=0,
        tiled=True,
    )
    padded_in = jnp.concatenate(
        [grad_in_rows.reshape(EXPERTS * capacity, width), jnp.zeros((1, width), jnp.float32)],
        axis=0,
    )
    grad_routed = grad_routed + jnp.sum(padded_in[slots].reshape(tok_rows, 2, width), axis=1)
    grad_gain_two = jnp.sum(grad_routed * normed_two, axis=0)
    scaled_two = grad_routed * gain_f[:, 1]
    grad_hidden = grad_out_rows + r_two * (
        scaled_two - normed_two * jnp.mean(scaled_two * normed_two, axis=-1, keepdims=True)
    )
    hid_low = grad_hidden.astype(jnp.bfloat16)
    grad_proj_w = jnp.dot(attended.T, hid_low, preferred_element_type=jnp.float32)
    grad_attended = jnp.dot(hid_low, w_proj.T, preferred_element_type=jnp.float32).astype(
        jnp.bfloat16
    )
    grad_heads = lax.all_to_all(
        grad_attended.reshape(tok_rows, seq_count, head_cols),
        "seq",
        split_axis=1,
        concat_axis=0,
        tiled=True,
    )
    grad_mixed = grad_heads.reshape(group_len, local_heads, HEAD_DIM)

    def back_block(carry, inputs):
        begin, log_rows = inputs
        masked, query_block = block_scores(begin)
        probs = jnp.exp(masked - log_rows[:, :, None])
        grad_block = lax.dynamic_slice_in_dim(grad_mixed, begin, block, 0)
        grad_p = jnp.einsum("qhd,khd->hqk", grad_block, values, preferred_element_type=jnp.float32)
        inner = jnp.sum(probs * grad_p, axis=-1, keepdims=True)
        grad_scores = (probs * (grad_p - inner)).astype(jnp.bfloat16)
        grad_query = (
            jnp.einsum("hqk,khd->qhd", grad_scores, keys, preferred_element_type=jnp.float32)
            * scale
        )
        grad_key = (
            carry[0]
            + jnp.einsum(
                "hqk,qhd->khd", grad_scores, query_block, preferred_element_type=jnp.float32
            )
            * scale
        )
        grad_value = carry[1] + jnp.einsum(
            "hqk,qhd->khd",
            probs.astype(jnp.bfloat16),
            grad_block,
            preferred_element_type=jnp.float32,
        )
        return ((grad_key, grad_value), grad_query)

    zero_heads = jnp.zeros((group_len, local_heads, HEAD_DIM), jnp.float32)
    (grad_keys, grad_values), grad_queries = lax.scan(
        back_block, (zero_heads, zero_heads), (begins, log_totals)
    )
    stacked = jnp.stack(
        [
            grad_queries.reshape(group_len, head_cols),
            grad_keys.reshape(group_len, head_cols),
            grad_values.reshape(group_len, head_cols),
        ],
        axis=1,
    )
    stacked = stacked.astype(jnp.bfloat16).reshape(group_len, 3, 1, head_cols)
    grad_back = lax.all_to_all(stacked, "seq", split_axis=0, concat_axis=2, tiled=True)
    grad_proj_rows = grad_back.reshape(tok_rows, 3 * width)
    grad_qkv_w = jnp.dot(normed_low.T, grad_proj_rows, preferred_element_type=jnp.float32)
    grad_normed = jnp.dot(grad_proj_rows, w_qkv.T, preferred_element_type=jnp.float32)
    grad_gain_one = jnp.sum(grad_normed * normed_one, axis=0)
    scaled_one = grad_normed * gain_f[:, 0]
    grad_x = grad_hidden + r_one * (
        scaled_one - normed_one * jnp.mean(scaled_one * normed_one, axis=-1, keepdims=True)
    )
    grad_gains = jnp.stack([grad_gain_one, grad_gain_two], axis=1)
    shard_qkv, shard_proj, shard_route, shard_gains = (
        lax.psum_scatter(
            grad_qkv_w.astype(jnp.bfloat16), "fsdp", scatter_dimension=0, tiled=True
        ).astype(jnp.float32),
        lax.psum_scatter(
            grad_proj_w.astype(jnp.bfloat16), "fsdp", scatter_dimension=0, tiled=True
        ).astype(jnp.float32),
        lax.psum_scatter(
            grad_route_w.astype(jnp.bfloat16), "fsdp", scatter_dimension=0, tiled=True
        ).astype(jnp.float32),
        lax.psum_scatter(
            grad_gains.astype(jnp.bfloat16), "fsdp", scatter_dimension=0, tiled=True
        ).astype(jnp.float32),
    )
    part_qkv, part_proj, part_expert = (
        lax.psum_scatter(
            shard_qkv.astype(jnp.bfloat16), ("dp", "seq"), scatter_dimension=1, tiled=True
        ).astype(jnp.float32),
        lax.psum_scatter(
            shard_proj.astype(jnp.bfloat16), ("dp", "seq"), scatter_dimension=1, tiled=True
        ).astype(jnp.float32),
        lax.psum_scatter(expert_shard, ("dp", "seq"), scatter_dimension=2, tiled=True).astype(
            jnp.float32
        ),
    )
    summed_qkv, summed_proj, summed_expert = (
        lax.all_gather(part_qkv.astype(jnp.bfloat16), ("dp", "seq"), axis=1, tiled=True).astype(
            part_qkv.dtype
        ),
        lax.all_gather(part_proj.astype(jnp.bfloat16), ("dp", "seq"), axis=1, tiled=True).astype(
            part_proj.dtype
        ),
        lax.all_gather(part_expert.astype(jnp.bfloat16), ("dp", "seq"), axis=2, tiled=True).astype(
            part_expert.dtype
        ),
    )
    summed_route, summed_gains = lax.psum((shard_route, shard_gains), ("dp", "seq"))
    return (
        block_out.astype(jnp.bfloat16)[None],
        grad_x.astype(jnp.bfloat16)[None],
        summed_qkv,
        summed_proj,
        summed_route,
        summed_gains,
        summed_expert,
    )


def solution(mesh):
    in_specs = (
        P(("dp", "fsdp"), "seq", None),
        P("fsdp", None),
        P("fsdp", None),
        P("fsdp", None),
        P("fsdp", None),
        P("fsdp", None, None),
        P(("dp", "fsdp"), "seq", None),
        P(("dp", "fsdp"), None),
        P(("dp", "fsdp"), "seq", None),
    )
    out_specs = (
        P(("dp", "fsdp"), "seq", None),
        P(("dp", "fsdp"), "seq", None),
        P("fsdp", None),
        P("fsdp", None),
        P("fsdp", None),
        P("fsdp", None),
        P("fsdp", None, None),
    )
    return jax.shard_map(shards, mesh=mesh, in_specs=in_specs, out_specs=out_specs, check_vma=False)
```

profile of v0, /device:TPU:0, one launch (start us, length us, event | category | flops | bytes accessed | tf_op | source)
XLA Modules:
  0.0 1859.5 jit_solution(3492848803113367879)
XLA Ops:
  33.3 49.0 %all-gather.7.cloned.1.call-done = bf16[768,2304]{1,0:T(8,128)(2,1)} async-done(((bf16[192,2304]{1,0:T(8,128)(2,1)}), bf16[768,2304]{1,0:T(8,128)(2,1)}) %all-gather.7.cloned.1.call-update) | async-done | bytes 3538960 | tf_op jit(solution)/shard_map/all_gather | solution.py:71
  157.0 65.0 %while.28 = (s32[]{:T(128)}, bf16[3,512,6,64]{1,3,2,0:T(8,128)(2,1)}, f32[3,6,512]{2,1,0:T(8,128)}, s32[3]{0:T(128)S(1)}, s32[1536]{0:T(1024)S(1)}, /*index=5*/b...) while((s32[]{:T(128)}, ...), condition=%wide.region_4.5_spmd.clone, body=%wide.region_1.4_spmd.clone.sunk | while | flops 1267923968 | bytes 63042744 | solution.py:123
  300.8 443.7 %all-gather.11.cloned.1.call-done = bf16[3072,4,1536]{2,0,1:T(8,128)(2,1)} async-done(((bf16[768,4,1536]{2,0,1:T(8,128)(2,1)}), bf16[3072,4,1536]{2,0,1:T(8,128)(2,1)}) %all-gather.11.cloned.1.call-update) | async-done | bytes 37748752 | tf_op jit(solution)/shard_map/all_gather | solution.py:144
  744.5 18.9 %fusion.56 = f32[4,384,3072]{2,1,0:T(8,128)} fusion(bf16[3072,4,1536]{2,0,1:T(8,128)(2,1)} %all-gather.11.cloned.1.call-done, bf16[4,384,768]{1,2,0:T(8,128)(2,1)S(1)} %copy-done.23, pred[4,384]{1,0:T(4,128)(4,1)S(1)} %copy-done.63), kind=kOutput, calls=%fused_computation.77 | convolution fusion | flops 7248936960 | bytes 40109568 | tf_op jit(solution)/shard_map/ecd,fed->ecf/dot_general | solution.py:40
  763.4 19.1 %convert_bitcast_fusion = bf16[3072,4,768]{0,2,1:T(8,128)(2,1)} fusion(bf16[4,384,768]{1,2,0:T(8,128)(2,1)S(1)} %copy-done.25, pred[4,384]{1,0:T(4,128)(4,1)S(1)} %copy-done.63, f32[4,384,3072]{2,1,0:T(8,128)} %fusion.56), kind=kOutput, calls=%fused_computation.68 | convolution fusion | flops 7300841472 | bytes 40109568 | tf_op jit(solution)/shard_map/ecf,ecd->fed/dot_general | solution.py:174
  782.5 25.0 %fusion.49 = bf16[4,384,3072]{2,1,0:T(8,128)(2,1)} fusion(f32[4,384,3072]{2,1,0:T(8,128)} %fusion.56, bf16[3072,4,1536]{2,0,1:T(8,128)(2,1)} %all-gather.11.cloned.1.call-done, bf16[4,384,768]{1,2,0:T(8,128)(2,1)} %copy.335, pred[4,384]{1,0:T(4,128)(4,1)S(1)} %copy-done.63), kind=kOutput, calls=%fused_computation.67 | convolution fusion | flops 7343308800 | bytes 49546752 | tf_op jit(solution)/shard_map/ecd,fed->ecf/dot_general | solution.py:54
  807.5 17.0 convert_bitcast_fusion.1
  824.5 25.8 %pad_maximum_fusion = bf16[3072,4,1536]{0,2,1:T(8,128)(2,1)} fusion(bf16[3072,4,768]{0,2,1:T(8,128)(2,1)} %convert_bitcast_fusion, bf16[3072,4,768]{0,2,1:T(8,128)(2,1)} %convert_bitcast_fusion.1), kind=kLoop, calls=%fused_computation.58 | loop fusion | flops 75497472 | bytes 75497472 | tf_op jit(solution)/shard_map/concatenate | solution.py:178
  851.8 18.4 fusion.52
  891.2 13.5 multiply_reduce_fusion.1
  908.0 17.1 fusion.54
  970.5 15.5 all-to-all-done.2
  994.5 176.0 %while.29 = (s32[]{:T(128)}, f32[1536,6,64]{0,2,1:T(8,128)S(1)}, f32[1536,6,64]{0,2,1:T(8,128)}, bf16[3,512,6,64]{1,3,2,0:T(8,128)(2,1)}, s32[3]{0:T(128)S(1)}, ...) while((s32[]{:T(128)}, f32[1536,6,64]{0,2,1:T(8,128)S(1)}, ...), condition=%wide.region_22.23_spmd.clone, body=%wide.region_20.22_spmd.clone.sunk | while | flops 3096968192 | bytes 245085472 | solution.py:235
  1018.4 14.7 multiply_reduce_fusion.8
  1076.8 15.0 multiply_reduce_fusion.8
  1091.8 13.5 multiply_convert_fusion.6
  1135.5 14.8 multiply_reduce_fusion.8
  1150.3 13.7 multiply_convert_fusion.6
  1194.4 50.4 %all-to-all-done.3 = bf16[1536,3,1,384]{3,1,2,0:T(4,128)(2,1)} async-done(((bf16[1536,3,1,384]{3,1,2,0:T(4,128)(2,1)}), bf16[1536,3,1,384]{3,1,2,0:T(4,128)(2,1)}, u32[]{:S(2)}, u32[]{:S(2)}) %all-to-all-start.3) | async-done | bytes 3538976 | tf_op jit(solution)/shard_map/all_to_all | solution.py:247
  1258.7 209.2 %reduce-scatter.21.cloned.1.call-done = bf16[768,4,1536]{0,2,1:T(8,128)(2,1)} async-done(((bf16[3072,4,1536]{0,2,1:T(8,128)(2,1)}), bf16[768,4,1536]{0,2,1:T(8,128)(2,1)}) %reduce-scatter.21.cloned.1.call-update) | async-done | bytes 9437200 | tf_op jit(solution)/shard_map/reduce_scatter | solution.py:177
  1479.7 21.4 %reduce-scatter.19.cloned.1.call-done = bf16[192,768]{1,0:T(8,128)(2,1)} async-done(((bf16[768,768]{1,0:T(8,128)(2,1)}), bf16[192,768]{1,0:T(8,128)(2,1)}) %reduce-scatter.19.cloned.1.call-update) | async-done | bytes 294928 | tf_op jit(solution)/shard_map/reduce_scatter | solution.py:261
  1503.0 65.4 %reduce-scatter.17.cloned.1.call-done = bf16[192,2304]{1,0:T(8,128)(2,1)} async-done(((bf16[768,2304]{1,0:T(8,128)(2,1)}), bf16[192,2304]{1,0:T(8,128)(2,1)}) %reduce-scatter.17.cloned.1.call-update) | async-done | bytes 884752 | tf_op jit(solution)/shard_map/reduce_scatter | solution.py:258
  1570.8 78.3 %reduce-scatter.23.cloned.1.call-done = bf16[768,4,192]{0,2,1:T(8,128)(2,1)} async-done(((bf16[768,4,1536]{0,2,1:T(8,128)(2,1)}), bf16[768,4,192]{0,2,1:T(8,128)(2,1)}) %reduce-scatter.23.cloned.1.call-update) | async-done | bytes 1179664 | tf_op jit(solution)/shard_map/reduce_scatter | solution.py:278
  1650.6 20.2 %reduce-scatter.29.cloned.1.call-done = bf16[192,4]{1,0:T(8,128)(2,1)} async-done(((bf16[768,4]{1,0:T(8,128)(2,1)}), bf16[192,4]{1,0:T(8,128)(2,1)}) %reduce-scatter.29.cloned.1.call-update) | async-done | bytes 1552
  1676.2 15.1 reduce-scatter.31.cloned.1.call-done
  1692.2 14.4 all-reduce.3
  1706.5 20.5 %reduce-scatter.27.cloned.1.call-done = bf16[96,192]{1,0:T(8,128)(2,1)} async-done(((bf16[768,192]{1,0:T(8,128)(2,1)}), bf16[96,192]{1,0:T(8,128)(2,1)}) %reduce-scatter.27.cloned.1.call-update) | async-done | bytes 36880
  1727.1 17.0 all_gather.31
  1745.0 23.0 %reduce-scatter.25.cloned.1.call-done = bf16[288,192]{1,0:T(8,128)(2,1)} async-done(((bf16[2304,192]{1,0:T(8,128)(2,1)}), bf16[288,192]{1,0:T(8,128)(2,1)}) %reduce-scatter.25.cloned.1.call-update) | async-done | bytes 110608
  1768.0 26.9 %all_gather.30 = bf16[192,2304]{0,1:T(8,128)(2,1)S(1)} all-gather(bf16[192,288]{0,1:T(8,128)(2,1)} %bitcast.212), channel_id=1, replica_groups=mesh['dp'=4,'seq'=2,'fsdp'=4] {'dp','seq'}, dimensions={1}, use_global_device_ids=true | all-gather | bytes 995328 | tf_op jit(solution)/shard_map/all_gather | solution.py:283
  1796.5 38.2 %all-gather.13.cloned.1.call-done = bf16[768,4,1536]{0,2,1:T(8,128)(2,1)} async-done(((bf16[768,4,192]{0,2,1:T(8,128)(2,1)}), bf16[768,4,1536]{0,2,1:T(8,128)(2,1)}) %all-gather.13.cloned.1.call-update) | async-done | bytes 9437200 | tf_op jit(solution)/shard_map/all_gather | solution.py:289
  1834.7 17.8 copy.352
  (364 shorter events, 479.0 us)
Async XLA Ops:
  7.2 75.2 %all-gather.7.cloned.1.call-start = ((), (), s32[]{:S(2)}) async-start(), calls=%async_computation.12 | async-start | bytes 4423680 | tf_op jit(solution)/shard_map/all_gather | solution.py:71
  7.9 263.5 %all-gather.9.cloned.1.call-start = ((), (), s32[]{:S(2)}) async-start(), calls=%async_computation.13 | async-start | bytes 1474560 | tf_op jit(solution)/shard_map/all_gather | solution.py:72
  8.6 735.9 %all-gather.11.cloned.1.call-start = ((), (), s32[]{:S(2)}) async-start(), calls=%async_computation.14 | async-start | bytes 47185920 | tf_op jit(solution)/shard_map/all_gather | solution.py:144
  18.0 13.8 copy-start.26
  32.4 50.0 %copy-start.12 = (bf16[1,768,768]{1,2,0:T(8,128)(2,1)}, bf16[1,768,768]{1,2,0:T(8,128)(2,1)S(1)}, u32[]{:S(2)}) copy-start(bf16[1,768,768]{1,2,0:T(8,128)(2,1)S(1)} %copy.309) | copy-start | bytes 3538948
  33.0 49.3 %copy-start.58 = (f32[768]{0:T(1024)}, f32[768]{0:T(1024)S(1)}, u32[]{:S(2)}) copy-start(f32[768]{0:T(1024)S(1)} %get-tuple-element.269) | copy-start | bytes 9220
  33.3 49.0 %copy-start.60 = (f32[768]{0:T(1024)}, f32[768]{0:T(1024)S(1)}, u32[]{:S(2)}) copy-start(f32[768]{0:T(1024)S(1)} %add_rsqrt_fusion.1) | copy-start | bytes 9220
  97.6 52.6 %all-to-all-start = ((bf16[768,3,2,384]{3,0,1,2:T(8,128)(2,1)}), bf16[768,3,2,384]{3,0,1,2:T(8,128)(2,1)S(1)}, u32[]{:S(2)}, u32[]{:S(2)}) async-start(bf16[768,3,2,384]{3,0,1,2:T(8,128)(2,1)} %copy.311), calls=%async_computation | async-start | bytes 7077888 | tf_op jit(solution)/shard_map/all_to_all | solution.py:83
  130.5 20.0 %copy-start.56 = (s32[1536]{0:T(1024)}, s32[1536]{0:T(1024)S(1)}, u32[]{:S(2)}) copy-start(s32[1536]{0:T(1024)S(1)} %fusion.98) | copy-start | bytes 18436
  221.9 13.6 copy-start.1
  221.9 13.6 copy-start.3
  221.9 13.6 copy-start.21
  247.4 19.1 %all-to-all-start.1 = ((bf16[2,2,147456]{2,1,0:T(2,128)(2,1)}), bf16[2,2,147456]{2,1,0:T(2,128)(2,1)}, u32[]{:S(2)}, u32[]{:S(2)}) async-start(bf16[2,2,147456]{2,1,0:T(2,128)(2,1)} %reshape.523), calls=%async_computation.1 | async-start | bytes 2359296 | tf_op jit(solution)/shard_map/all_to_all | solution.py:125
  251.8 1216.1 %reduce-scatter.21.cloned.1.call-start = ((), (), s32[]{:S(2)}) async-start(), calls=%async_computation.17 | async-start | bytes 47185920 | tf_op jit(solution)/shard_map/reduce_scatter | solution.py:177
  276.0 7.8 copy-start.8
  296.4 448.1 %copy-start.23 = (bf16[4,384,768]{1,2,0:T(8,128)(2,1)S(1)}, bf16[4,384,768]{1,2,0:T(8,128)(2,1)}, u32[]{:S(2)}) copy-start(bf16[4,384,768]{1,2,0:T(8,128)(2,1)} %copy.326) | copy-start | bytes 7077892
  296.4 448.1 %copy-start.63 = (pred[4,384]{1,0:T(4,128)(4,1)S(1)}, pred[4,384]{1,0:T(4,128)(4,1)}, u32[]{:S(2)}) copy-start(pred[4,384]{1,0:T(4,128)(4,1)} %gt.8) | copy-start | bytes 4612
  744.5 18.9 %copy-start.25 = (bf16[4,384,768]{1,2,0:T(8,128)(2,1)S(1)}, bf16[4,384,768]{1,2,0:T(8,128)(2,1)}, u32[]{:S(2)}) copy-start(bf16[4,384,768]{1,2,0:T(8,128)(2,1)} %copy.335) | copy-start | bytes 7077892
  966.8 19.1 %all-to-all-start.2 = ((bf16[768,2,384]{0,2,1:T(8,128)(2,1)}), bf16[768,2,384]{0,2,1:T(8,128)(2,1)S(1)}, u32[]{:S(2)}, u32[]{:S(2)}) async-start(bf16[768,2,384]{0,2,1:T(8,128)(2,1)} %bitcast.23), calls=%async_computation.2 | async-start | bytes 2359296 | tf_op jit(solution)/shard_map/all_to_all | solution.py:198
  1033.1 13.4 copy-start.29
  1091.8 13.5 copy-start.29
  1150.3 13.7 copy-start.29
  1186.1 58.8 %all-to-all-start.3 = ((bf16[1536,3,1,384]{3,1,2,0:T(4,128)(2,1)}), bf16[1536,3,1,384]{3,1,2,0:T(4,128)(2,1)}, u32[]{:S(2)}, u32[]{:S(2)}) async-start(bf16[1536,3,1,384]{3,1,2,0:T(4,128)(2,1)} %copy.341), calls=%async_computation.3 | async-start | bytes 9437184 | tf_op jit(solution)/shard_map/all_to_all | solution.py:247
  1192.1 308.9 %reduce-scatter.19.cloned.1.call-start = ((), (), s32[]{:S(2)}) async-start(), calls=%async_computation.16 | async-start | bytes 1474560 | tf_op jit(solution)/shard_map/reduce_scatter | solution.py:261
  1194.4 374.1 %reduce-scatter.17.cloned.1.call-start = ((), (), s32[]{:S(2)}) async-start(), calls=%async_computation.15 | async-start | bytes 4423680 | tf_op jit(solution)/shard_map/reduce_scatter | solution.py:258
  1258.6 390.5 %reduce-scatter.23.cloned.1.call-start = ((), (), s32[]{:S(2)}) async-start(), calls=%async_computation.18 | async-start | bytes 10616832 | tf_op jit(solution)/shard_map/reduce_scatter | solution.py:278
  1468.0 202.9 %reduce-scatter.29.cloned.1.call-start = ((), (), s32[]{:S(2)}) async-start(), calls=%async_computation.22 | async-start | bytes 245760
  1471.1 220.1 %reduce-scatter.31.cloned.1.call-start = ((), (), s32[]{:S(2)}) async-start(), calls=%async_computation.23 | async-start | bytes 245760
  1479.6 247.5 %reduce-scatter.27.cloned.1.call-start = ((), (), s32[]{:S(2)}) async-start(), calls=%async_computation.21 | async-start | bytes 442368
  1502.9 146.2 %copy-start.18 = (bf16[1,768,768]{1,2,0:T(8,128)(2,1)S(1)}, bf16[1,768,768]{1,2,0:T(8,128)(2,1)}, u32[]{:S(2)}) copy-start(bf16[1,768,768]{1,2,0:T(8,128)(2,1)} %get-tuple-element.320) | copy-start | bytes 3538948
  1502.9 265.1 %reduce-scatter.25.cloned.1.call-start = ((), (), s32[]{:S(2)}) async-start(), calls=%async_computation.20 | async-start | bytes 1327104
  1570.8 263.9 %all-gather.13.cloned.1.call-start = ((), (), s32[]{:S(2)}) async-start(), calls=%async_computation.19 | async-start | bytes 10616832 | tf_op jit(solution)/shard_map/all_gather | solution.py:289
  (58 other events, 195.5 us)
Sparse Core Ops, SparseCore 0:
  9.6 72.6 all-gather.6
  83.9 29.0 all-gather.8
  115.2 629.2 all-gather.10
  850.5 617.4 reduce-scatter.20
  1470.8 30.2 reduce-scatter.18
  1503.3 65.0 reduce-scatter.16
  1572.3 76.7 reduce-scatter.22
  1651.5 19.3 reduce-scatter.28
  1673.7 17.5 reduce-scatter.30
  1695.1 31.9 reduce-scatter.26
  1731.2 36.7 reduce-scatter.24
  1769.8 64.8 all-gather.12
where the time goes:
time: 1870 us; the launch traced here: 1860 us
  waiting for transfers between devices  1050 us (56%)
  matrix products  284 us (15%)
  local copies, waits for them, and re-layouts  251 us (13%)
  other arithmetic  143 us (8%)
  blocking collectives  83.3 us (4%)
  starting transfers between devices  18.8 us (1%)
    all_gather x1, waiting for transfers between devices, shards(): piece = lax.all_gather(expert_w, 'fsdp', axis=0, tiled=True)  444 us
    reduce_scatter x1, waiting for transfers between devices, shards(): lax.psum_scatter(jnp.concatenate([grad_first, grad_second], axis=2).astyp...  209 us
    unnamed x16, waiting for transfers between devices  80.4 us
    reduce_scatter x1, waiting for transfers between devices, shards(): lax.psum_scatter(expert_shard, ('dp', 'seq'), scatter_dimension=2, tiled=...  78.3 us
    reduce_scatter x1, waiting for transfers between devices, shards(): lax.psum_scatter(grad_qkv_w.astype(jnp.bfloat16), 'fsdp', scatter_dimensi...  65.4 us
    unnamed x149, local copies, waits for them, and re-layouts  58 us
    all_to_all x1, waiting for transfers between devices, shards(): lax.all_to_all(stacked, 'seq', split_axis=0, concat_axis=2, tiled=True)  50.4 us
    all_gather x1, waiting for transfers between devices, shards(): lax.all_gather(attn_in, 'fsdp', axis=0, tiled=True)  49 us
  transfers between devices with their start and end apart: 16, of which 13 were waited for; matrix products, arithmetic and copies ran while one was open for 28% of the time, Pallas kernels for 0%

commit v1 on v0

--- a/solution.py
+++ b/solution.py
@@ -10,6 +10,28 @@
 EPSILON = 1e-06
 NEGATIVE = -1e30
 HIGH = lax.Precision.HIGHEST
+
+
+def joined_along(blocks, dim):
+    dims = list(blocks.shape[1:])
+    dims[dim] *= blocks.shape[0]
+    return jnp.moveaxis(blocks, 0, dim).reshape(dims)
+
+
+def grow_blocks(x, axis):
+    count = lax.axis_size(axis)
+    pieces = x[None]
+    for level in range(count.bit_length() - 1):
+        apart = 1 << level
+        other = lax.ppermute(pieces, axis, [(i, i ^ apart) for i in range(count)])
+        both = jnp.stack([pieces, other])
+        upper = lax.axis_index(axis) >> level & 1
+        pieces = jnp.where(upper == 0, both, both[::-1]).reshape(-1, *x.shape)
+    return pieces
+
+
+def collect(array, axis, dim):
+    return joined_along(grow_blocks(array, axis), dim)
 
 
 def route(choose, capacity, experts_count):
@@ -286,9 +308,7 @@
         lax.all_gather(part_proj.astype(jnp.bfloat16), ("dp", "seq"), axis=1, tiled=True).astype(
             part_proj.dtype
         ),
-        lax.all_gather(part_expert.astype(jnp.bfloat16), ("dp", "seq"), axis=2, tiled=True).astype(
-            part_expert.dtype
-        ),
+        collect(part_expert.astype(jnp.bfloat16), ("dp", "seq"), 2).astype(part_expert.dtype),
     )
     summed_route, summed_gains = lax.psum((shard_route, shard_gains), ("dp", "seq"))
     return (

time: 1870 us -> 2020 us (1.080)
  waiting for transfers between devices: 1050 us -> 1120 us
  other arithmetic: 143 us -> 178 us
  blocking collectives: 83.3 us -> 107 us
    reduce_scatter x1, waiting for transfers between devices: 209 us -> 476 us  [shards(): lax.psum_scatter(jnp.concatenate([grad_first, grad_second], axis=2).astyp...]
    reduce_scatter x1, waiting for transfers between devices: 78.3 us -> 0.02 us  [shards(): lax.psum_scatter(expert_shard, ('dp', 'seq'), scatter_dimension=2, tiled=...]
    reduce_scatter x1, waiting for transfers between devices: 65.4 us -> 11.4 us  [shards(): lax.psum_scatter(grad_qkv_w.astype(jnp.bfloat16), 'fsdp', scatter_dimensi...]
    all_gather x1 -> x0, waiting for transfers between devices: 38.2 us -> none  [shards(): lax.all_gather(part_expert.astype(jnp.bfloat16), ('dp', 'seq'), axis=2, t...]
    unnamed x16 -> x15, waiting for transfers between devices: 80.4 us -> 46.8 us
    ppermute x0 -> x3, waiting for transfers between devices: none -> 31.5 us  [grow_blocks(): other = lax.ppermute(pieces, axis, [(i, i ^ apart) for i in range(count)])]
    psum x1, blocking collectives: 14.4 us -> 45.8 us  [shards(): lax.psum((shard_route, shard_gains), ('dp', 'seq'))]
    reduce_scatter x1, waiting for transfers between devices: 21.4 us -> 0.02 us  [shards(): lax.psum_scatter(grad_proj_w.astype(jnp.bfloat16), 'fsdp', scatter_dimens...]
  transfers between devices with their start and end apart: 16 -> 18, of which waited for: 13 -> 11; matrix products, arithmetic and copies ran while one was open for 28% -> 27% of each run, Pallas kernels for 0% -> 0%
where the time goes in v1:
time: 2020 us; the launch traced here: 2010 us
  waiting for transfers between devices  1120 us (55%)
  matrix products  285 us (14%)
  local copies, waits for them, and re-layouts  270 us (13%)
  other arithmetic  178 us (9%)
  blocking collectives  107 us (5%)
  starting transfers between devices  21 us (1%)
    reduce_scatter x1, waiting for transfers between devices, shards(): lax.psum_scatter(jnp.concatenate([grad_first, grad_second], axis=2).astyp...  476 us
    all_gather x1, waiting for transfers between devices, shards(): piece = lax.all_gather(expert_w, 'fsdp', axis=0, tiled=True)  444 us
    unnamed x147, local copies, waits for them, and re-layouts  63.7 us
    all_to_all x1, waiting for transfers between devices, shards(): lax.all_to_all(stacked, 'seq', split_axis=0, concat_axis=2, tiled=True)  50.9 us
    all_gather x1, waiting for transfers between devices, shards(): lax.all_gather(attn_in, 'fsdp', axis=0, tiled=True)  49 us
    unnamed x15, waiting for transfers between devices  46.8 us
    psum x1, blocking collectives, shards(): lax.psum((shard_route, shard_gains), ('dp', 'seq'))  45.8 us
    dot_general x3, matrix products, back_block(): jnp.einsum('qhd,khd->hqk', grad_block, values, preferred_element_type=jnp...  45 us
  transfers between devices with their start and end apart: 18, of which 11 were waited for; matrix products, arithmetic and copies ran while one was open for 27% of the time, Pallas kernels for 0%

profile of v1, /device:TPU:0, one launch (start us, length us, event | category | flops | bytes accessed | tf_op | source)
XLA Modules:
  0.0 2013.1 jit_solution(11664779237122675888)
XLA Ops:
  18.7 13.0 all-gather
  33.3 49.0 %all-gather.6.cloned.1.call-done = bf16[768,2304]{1,0:T(8,128)(2,1)} async-done(((bf16[192,2304]{1,0:T(8,128)(2,1)}), bf16[768,2304]{1,0:T(8,128)(2,1)}) %all-gather.6.cloned.1.call-update) | async-done | bytes 3538960 | tf_op jit(solution)/shard_map/all_gather | solution.py:93
  157.0 65.0 %while.28 = (s32[]{:T(128)}, bf16[3,512,6,64]{1,3,2,0:T(8,128)(2,1)}, f32[3,6,512]{2,1,0:T(8,128)}, s32[3]{0:T(128)S(1)}, s32[1536]{0:T(1024)S(1)}, /*index=5*/b...) while((s32[]{:T(128)}, ...), condition=%wide.region_4.5_spmd.clone, body=%wide.region_1.4_spmd.clone.sunk | while | flops 1267923968 | bytes 63042744 | solution.py:145
  300.9 443.7 %all-gather.10.cloned.1.call-done = bf16[3072,4,1536]{2,0,1:T(8,128)(2,1)} async-done(((bf16[768,4,1536]{2,0,1:T(8,128)(2,1)}), bf16[3072,4,1536]{2,0,1:T(8,128)(2,1)}) %all-gather.10.cloned.1.call-update) | async-done | bytes 37748752 | tf_op jit(solution)/shard_map/all_gather | solution.py:166
  744.5 18.9 fusion.56
  763.4 19.1 convert_bitcast_fusion
  782.5 25.0 %fusion.49 = bf16[4,384,3072]{2,1,0:T(8,128)(2,1)} fusion(f32[4,384,3072]{2,1,0:T(8,128)} %fusion.56, bf16[3072,4,1536]{2,0,1:T(8,128)(2,1)} %all-gather.10.cloned.1.call-done, bf16[4,384,768]{1,2,0:T(8,128)(2,1)} %copy.342, pred[4,384]{1,0:T(4,128)(4,1)S(1)} %copy-done.62), kind=kOutput, calls=%fused_computation.67 | convolution fusion | flops 7343308800 | bytes 49546752 | tf_op jit(solution)/shard_map/ecd,fed->ecf/dot_general | solution.py:76
  807.5 17.0 convert_bitcast_fusion.1
  824.5 25.8 %pad_maximum_fusion = bf16[3072,4,1536]{0,2,1:T(8,128)(2,1)} fusion(bf16[3072,4,768]{0,2,1:T(8,128)(2,1)} %convert_bitcast_fusion, bf16[3072,4,768]{0,2,1:T(8,128)(2,1)} %convert_bitcast_fusion.1), kind=kLoop, calls=%fused_computation.58 | loop fusion | flops 75497472 | bytes 75497472 | tf_op jit(solution)/shard_map/concatenate | solution.py:200
  851.8 18.4 fusion.52
  891.2 13.5 multiply_reduce_fusion.1
  908.0 17.1 fusion.54
  970.5 15.5 all-to-all-done.2
  992.1 475.8 %reduce-scatter.21.cloned.1.call-done = bf16[768,4,1536]{0,2,1:T(8,128)(2,1)} async-done(((bf16[3072,4,1536]{0,2,1:T(8,128)(2,1)}), bf16[768,4,1536]{0,2,1:T(8,128)(2,1)}) %reduce-scatter.21.cloned.1.call-update) | async-done | bytes 9437200 | tf_op jit(solution)/shard_map/reduce_scatter | solution.py:199
  1469.2 179.4 %while.29 = (s32[]{:T(128)}, f32[1536,6,64]{0,2,1:T(8,128)S(1)}, f32[1536,6,64]{0,2,1:T(8,128)}, bf16[3,512,6,64]{1,3,2,0:T(8,128)(2,1)}, s32[3]{0:T(128)S(1)}, ...) while((s32[]{:T(128)}, f32[1536,6,64]{0,2,1:T(8,128)S(1)}, ...), condition=%wide.region_22.23_spmd.clone, body=%wide.region_20.22_spmd.clone.sunk | while | flops 3096968192 | bytes 245085472 | solution.py:257
  1496.0 15.5 multiply_reduce_fusion.8
  1511.5 13.9 multiply_convert_fusion.6
  1555.7 14.8 multiply_reduce_fusion.8
  1570.5 13.3 multiply_convert_fusion.6
  1614.0 14.8 multiply_reduce_fusion.8
  1628.8 13.3 multiply_convert_fusion.6
  1672.6 50.9 %all-to-all-done.3 = bf16[1536,3,1,384]{3,1,2,0:T(4,128)(2,1)} async-done(((bf16[1536,3,1,384]{3,1,2,0:T(4,128)(2,1)}), bf16[1536,3,1,384]{3,1,2,0:T(4,128)(2,1)}, u32[]{:S(2)}, u32[]{:S(2)}) %all-to-all-start.3) | async-done | bytes 3538976 | tf_op jit(solution)/shard_map/all_to_all | solution.py:269
  1737.6 26.6 %collective-permute-done = bf16[1,768,4,192]{1,3,2,0:T(8,128)(2,1)S(1)} collective-permute-done((bf16[1,768,4,192]{1,3,2,0:T(8,128)(2,1)}, bf16[1,768,4,192]{1,3,2,0:T(8,128)(2,1)S(1)}, u32[]{:S(2)}, u32[]{:S(2)}) %collective-permute-start) | collective-permute-done | bytes 1179680 | tf_op jit(solution)/shard_map/ppermute | solution.py:26
  1808.8 17.9 reduce-scatter.29.cloned.1.call-done
  1833.2 13.3 reduce-scatter.31.cloned.1.call-done
  1847.3 45.8 %all-reduce.3 = (f32[192,4]{0,1:T(4,128)}, f32[192,2]{0,1:T(2,128)}) all-reduce(bf16[192,4]{0,1:T(4,128)(2,1)S(1)} %copy.371, bf16[192,2]{0,1:T(2,128)(2,1)S(1)} %copy.373), channel_id=1, replica_groups=mesh['dp'=4,'seq'=2,'fsdp'=4] {'dp','seq'}, use_global_device_ids=true, to_apply=%region_29.30 | all-reduce | flops 1152 | bytes 6912 | tf_op jit(solution)/shard_map/psum | solution.py:313
  1893.1 15.7 all_gather.28
  1909.8 14.1 reduce-scatter.25.cloned.1.call-done
  1923.9 20.6 %all_gather.27 = bf16[192,2304]{0,1:T(8,128)(2,1)S(1)} all-gather(bf16[192,288]{0,1:T(8,128)(2,1)} %bitcast.232), channel_id=1, replica_groups=mesh['dp'=4,'seq'=2,'fsdp'=4] {'dp','seq'}, dimensions={1}, use_global_device_ids=true | all-gather | bytes 995328 | tf_op jit(solution)/shard_map/all_gather | solution.py:305
  1954.4 16.8 fusion.58
  1971.2 12.6 copy.355
  1983.8 22.6 %copy.360 = f32[768,4,1536]{2,1,0:T(4,128)} copy(f32[768,4,1536]{0,2,1:T(8,128)} %bitcast.210) | data formatting | bytes 37748736
  (372 shorter events, 491.4 us)
Async XLA Ops:
  7.2 75.2 %all-gather.6.cloned.1.call-start = ((), (), s32[]{:S(2)}) async-start(), calls=%async_computation.12 | async-start | bytes 4423680 | tf_op jit(solution)/shard_map/all_gather | solution.py:93
  7.9 263.5 %all-gather.8.cloned.1.call-start = ((), (), s32[]{:S(2)}) async-start(), calls=%async_computation.13 | async-start | bytes 1474560 | tf_op jit(solution)/shard_map/all_gather | solution.py:94
  8.6 735.9 %all-gather.10.cloned.1.call-start = ((), (), s32[]{:S(2)}) async-start(), calls=%async_computation.14 | async-start | bytes 47185920 | tf_op jit(solution)/shard_map/all_gather | solution.py:166
  18.0 13.8 copy-start.25
  32.4 50.0 %copy-start.12 = (bf16[1,768,768]{1,2,0:T(8,128)(2,1)}, bf16[1,768,768]{1,2,0:T(8,128)(2,1)S(1)}, u32[]{:S(2)}) copy-start(bf16[1,768,768]{1,2,0:T(8,128)(2,1)S(1)} %copy.316) | copy-start | bytes 3538948
  33.0 49.3 %copy-start.57 = (f32[768]{0:T(1024)}, f32[768]{0:T(1024)S(1)}, u32[]{:S(2)}) copy-start(f32[768]{0:T(1024)S(1)} %get-tuple-element.269) | copy-start | bytes 9220
  33.3 49.0 %copy-start.59 = (f32[768]{0:T(1024)}, f32[768]{0:T(1024)S(1)}, u32[]{:S(2)}) copy-start(f32[768]{0:T(1024)S(1)} %add_rsqrt_fusion.1) | copy-start | bytes 9220
  97.6 52.6 %all-to-all-start = ((bf16[768,3,2,384]{3,0,1,2:T(8,128)(2,1)}), bf16[768,3,2,384]{3,0,1,2:T(8,128)(2,1)S(1)}, u32[]{:S(2)}, u32[]{:S(2)}) async-start(bf16[768,3,2,384]{3,0,1,2:T(8,128)(2,1)} %copy.318), calls=%async_computation | async-start | bytes 7077888 | tf_op jit(solution)/shard_map/all_to_all | solution.py:105
  130.5 20.0 copy-start.55
  221.9 13.6 copy-start.1
  221.9 13.6 copy-start.3
  221.9 13.6 copy-start.20
  247.4 19.1 all-to-all-start.1
  251.8 1216.1 %reduce-scatter.21.cloned.1.call-start = ((), (), s32[]{:S(2)}) async-start(), calls=%async_computation.17 | async-start | bytes 47185920 | tf_op jit(solution)/shard_map/reduce_scatter | solution.py:199
  296.4 448.1 %copy-start.23 = (bf16[4,384,768]{1,2,0:T(8,128)(2,1)S(1)}, bf16[4,384,768]{1,2,0:T(8,128)(2,1)}, u32[]{:S(2)}) copy-start(bf16[4,384,768]{1,2,0:T(8,128)(2,1)} %copy.333) | copy-start | bytes 7077892
  296.4 448.1 %copy-start.62 = (pred[4,384]{1,0:T(4,128)(4,1)S(1)}, pred[4,384]{1,0:T(4,128)(4,1)}, u32[]{:S(2)}) copy-start(pred[4,384]{1,0:T(4,128)(4,1)} %gt.8) | copy-start | bytes 4612
  744.5 18.9 copy-start.24
  966.8 19.1 all-to-all-start.2
  970.4 766.8 %reduce-scatter.23.cloned.1.call-start = ((), (), s32[]{:S(2)}) async-start(), calls=%async_computation.18 | async-start | bytes 10616832 | tf_op jit(solution)/shard_map/reduce_scatter | solution.py:300
  1511.5 13.9 copy-start.28
  1570.5 13.3 copy-start.28
  1664.2 59.2 %all-to-all-start.3 = ((bf16[1536,3,1,384]{3,1,2,0:T(4,128)(2,1)}), bf16[1536,3,1,384]{3,1,2,0:T(4,128)(2,1)}, u32[]{:S(2)}, u32[]{:S(2)}) async-start(bf16[1536,3,1,384]{3,1,2,0:T(4,128)(2,1)} %copy.348), calls=%async_computation.3 | async-start | bytes 9437184 | tf_op jit(solution)/shard_map/all_to_all | solution.py:269
  1670.3 120.3 %reduce-scatter.19.cloned.1.call-start = ((), (), s32[]{:S(2)}) async-start(), calls=%async_computation.16 | async-start | bytes 1474560 | tf_op jit(solution)/shard_map/reduce_scatter | solution.py:283
  1672.5 131.5 %reduce-scatter.17.cloned.1.call-start = ((), (), s32[]{:S(2)}) async-start(), calls=%async_computation.15 | async-start | bytes 4423680 | tf_op jit(solution)/shard_map/reduce_scatter | solution.py:280
  1737.1 89.5 %reduce-scatter.29.cloned.1.call-start = ((), (), s32[]{:S(2)}) async-start(), calls=%async_computation.21 | async-start | bytes 245760
  1737.2 26.9 %collective-permute-start = (bf16[1,768,4,192]{1,3,2,0:T(8,128)(2,1)}, bf16[1,768,4,192]{1,3,2,0:T(8,128)(2,1)S(1)}, u32[]{:S(2)}, u32[]{:S(2)}) collective-permute-start(bf16[1,768,4,192]{1,3,2,0:T(8,128)(2,1)} %bitcast.229), channel_id=1, source_target_pairs={{0,4},{4,0},{8,12},{12,8},{16,20},{20,16},{24,28},{28,24},{1,5},{5... | collective-permute-start | bytes 3538952 | tf_op jit(solution)/shard_map/ppermute | solution.py:26
  1767.7 4.9 collective-permute-start.1
  1778.1 168.0 %collective-permute-start.2 = (bf16[4,768,4,192]{1,3,2,0:T(8,128)(2,1)}, bf16[4,768,4,192]{1,3,2,0:T(8,128)(2,1)}, u32[]{:S(2)}, u32[]{:S(2)}) collective-permute-start(bf16[4,768,4,192]{1,3,2,0:T(8,128)(2,1)} %bitcast.42), channel_id=1, source_target_pairs={{0,16},{4,20},{8,24},{12,28},{16,0},{20,4},{24,8},{28,12},{1,17},{... | collective-permute-start | bytes 14155784 | tf_op jit(solution)/shard_map/ppermute | solution.py:26
  1781.7 64.8 %reduce-scatter.31.cloned.1.call-start = ((), (), s32[]{:S(2)}) async-start(), calls=%async_computation.22 | async-start | bytes 245760
  1790.5 102.6 %reduce-scatter.27.cloned.1.call-start = ((), (), s32[]{:S(2)}) async-start(), calls=%async_computation.20 | async-start | bytes 442368
  1792.5 35.0 %copy-start.18 = (f32[768,768]{0,1:T(8,128)S(1)}, f32[768,768]{0,1:T(8,128)}, u32[]{:S(2)}) copy-start(f32[768,768]{0,1:T(8,128)} %copy-done.16) | copy-start | bytes 7077892
  1792.5 131.4 %reduce-scatter.25.cloned.1.call-start = ((), (), s32[]{:S(2)}) async-start(), calls=%async_computation.19 | async-start | bytes 1327104
  (59 other events, 222.3 us)
Sparse Core Ops, SparseCore 0:
  9.6 72.6 all-gather.5
  83.9 29.0 all-gather.7
  115.2 629.2 all-gather.9
  850.5 617.4 reduce-scatter.20
  1471.7 77.5 reduce-scatter.22
  1673.8 30.7 reduce-scatter.18
  1737.3 66.7 reduce-scatter.16
  1806.9 19.6 reduce-scatter.28
  1828.9 17.5 reduce-scatter.30
  1850.2 32.8 reduce-scatter.26
  1886.7 37.1 reduce-scatter.24
